TPU v7x, 128 devices: a whole 4x4x4 slice. The times are simulated.
128 devices in a mesh: ctx: 32 (over y_hi, x, z), fsdp: 4 (over y_lo, core).
Axes of the slice: x: 4, y: 4 (y_hi: 2, y_lo: 2; y = y_hi * 2 + y_lo), z: 4, core: 2. Of those that a mesh axis runs over, the one named last changes fastest.
Arguments:
- layer_input: bfloat16 [4, 4096, 1024], P('fsdp', 'ctx'), may hold values from -6 to 6
- cotangent: bfloat16 [4, 4096, 1024], P('fsdp', 'ctx'), may hold values from -6 to 6
- block_order: int32 [4, 64], P('fsdp'), may hold values from 0 to 63, as said below
- query_weight: bfloat16 [1024, 2048], P('fsdp'), may hold values from -0.1875 to 0.1875
- key_projection: bfloat16 [1024, 1024], P('fsdp'), may hold values from -0.1875 to 0.1875
- value_projection: bfloat16 [1024, 1024], P('fsdp'), may hold values from -0.1875 to 0.1875
- output_weight: bfloat16 [2048, 1024], P('fsdp'), may hold values from -0.75 to 0.75
- gate_weight: bfloat16 [1024, 3072], P('fsdp'), may hold values from -0.1875 to 0.1875
- up_weight: bfloat16 [1024, 3072], P('fsdp'), may hold values from -0.1875 to 0.1875
- down_weight: bfloat16 [3072, 1024], P('fsdp'), may hold values from -0.109375 to 0.109375
- first_gain: float32 [1024], replicated, may hold values from 0.5 to 1.5
- second_gain: float32 [1024], replicated, may hold values from 0.5 to 1.5
- query_gain: float32 [128], replicated, may hold values from 0.25 to 1.75
- key_norm_gain: float32 [128], replicated, may hold values from 0.25 to 1.75
Outputs:
- layer_output: bfloat16 [4, 4096, 1024], P('fsdp', 'ctx')
- input_gradient: float32 [4, 4096, 1024], P('fsdp', 'ctx')
- query_weight_gradient: float32 [1024, 2048], P('fsdp')
- key_weight_gradient: float32 [1024, 1024], P('fsdp')
- value_weight_gradient: float32 [1024, 1024], P('fsdp')
- output_weight_gradient: float32 [2048, 1024], P('fsdp')
- gate_weight_gradient: float32 [1024, 3072], P('fsdp')
- up_weight_gradient: float32 [1024, 3072], P('fsdp')
- down_weight_gradient: float32 [3072, 1024], P('fsdp')
- first_gain_gradient: float32 [1024], P('fsdp')
- second_gain_gradient: float32 [1024], P('fsdp')
- query_gain_gradient: float32 [128], P('fsdp')
- key_gain_gradient: float32 [128], P('fsdp')
Inputs may be any that keep to these rules, and one draw needn't show every extreme that they name: Each row of block_order names every block of 64 positions of its sequence exactly once; the two blocks of rows 2 c and 2 c + 1 are mirrored, block b together with block 2 * 32 - 1 - b, in either order.
All inputs are finite; a program needn't handle non-finite values.
Results may differ from a plain program's by a relative error of at most 0.034.
Values may be sent and summed in bfloat16 or wider, within the bound.
No kernel may reach another device: no remote copies, remote signals or barrier semaphores. Data moves between devices by JAX's collectives and lax.ppermute only.
A program may use at most 320 MiB of HBM per device.

v0:
```python
import math
import jax
import jax.numpy as jnp
from jax import lax
from jax.sharding import PartitionSpec as P

HQ = 16
KEY_VALUE_HEADS = 8
HEAD_SIZE = 128
CTX = ("yh", "x", "z")
FSDP = ("yl", "c")
EPSILON = 1e-06
THETA = 1000000.0
MASKED = -1e30


def rms_apply(values, norm_gain):
    row_scale = lax.rsqrt(jnp.mean(values * values, axis=-1, keepdims=True) + EPSILON)
    normed = values * row_scale
    return (normed * norm_gain, normed, row_scale)


def root_mean_square_backward(gradient, normed, row_scale, norm_gain):
    normed_grad = gradient * norm_gain
    return row_scale * (
        normed_grad - normed * jnp.mean(normed_grad * normed, axis=-1, keepdims=True)
    )


def rope_tables(positions, head_width):
    half_width = head_width // 2
    inverse_freq = jnp.power(THETA, -2.0 * jnp.arange(half_width, dtype=jnp.float32) / head_width)
    angles = positions.astype(jnp.float32)[:, None] * inverse_freq[None, :]
    return (jnp.cos(angles)[:, None, :], jnp.sin(angles)[:, None, :])


def rotary_apply(values, cosine_table, sine_values_table):
    half_width = values.shape[-1] // 2
    front_half = values[..., :half_width]
    back_half = values[..., half_width:]
    return jnp.concatenate(
        [
            front_half * cosine_table - back_half * sine_values_table,
            back_half * cosine_table + front_half * sine_values_table,
        ],
        axis=-1,
    )


def rotary_backward(gradient, cosine_table, sine_values_table):
    half_width = gradient.shape[-1] // 2
    front_half = gradient[..., :half_width]
    back_half = gradient[..., half_width:]
    return jnp.concatenate(
        [
            front_half * cosine_table + back_half * sine_values_table,
            back_half * cosine_table - front_half * sine_values_table,
        ],
        axis=-1,
    )


def left_dot(left_side, right_side):
    return lax.dot_general(
        left_side, right_side, (((0,), (0,)), ((), ())), preferred_element_type=jnp.float32
    )


def right_dot(left_side, right_side):
    return lax.dot_general(
        left_side, right_side, (((1,), (1,)), ((), ())), preferred_element_type=jnp.float32
    )


def gather_fsdp(values):
    across = lax.all_gather(values, "yl", axis=0, tiled=False)
    both = lax.all_gather(across, "c", axis=1, tiled=False)
    return both.reshape((-1,) + values.shape[1:])


def reduce_ctx(shards):
    flat = jnp.concatenate([s.astype(jnp.bfloat16).reshape(-1) for s in shards])
    lanes = 128
    step = 256 * lanes
    padded = -(-flat.shape[0] // step) * step
    flat = jnp.pad(flat, (0, padded - flat.shape[0])).reshape(padded // lanes, lanes)
    part = lax.psum_scatter(flat, "z", scatter_dimension=0, tiled=True)
    part = lax.psum_scatter(part, "x", scatter_dimension=0, tiled=True)
    part = lax.psum(part, "yh")
    part = lax.all_gather(part, "x", axis=0, tiled=True)
    full = lax.all_gather(part, "z", axis=0, tiled=True).reshape(-1)
    out = []
    at = 0
    for s in shards:
        out.append(full[at : at + s.size].reshape(s.shape).astype(jnp.float32))
        at += s.size
    return tuple(out)


def on_device(
    layer_input,
    cotangent,
    block_order,
    query_weight,
    key_projection,
    value_projection,
    output_weight,
    gate_weight,
    up_weight,
    down_weight,
    first_gain,
    second_gain,
    query_gain,
    key_norm_gain,
):
    local_rows = layer_input.shape[1]
    block_rows = local_rows // 2
    ctx_size = lax.axis_size(CTX)
    halves = ctx_size // HQ
    half_devices = ctx_size // halves
    order_row = block_order[0]
    device_place = lax.axis_index(CTX)
    my_half = device_place // half_devices
    all_positions = (
        order_row[:, None] * block_rows + jnp.arange(block_rows, dtype=jnp.int32)[None, :]
    ).reshape(-1)
    own_positions = lax.dynamic_slice_in_dim(all_positions, device_place * local_rows, local_rows)
    cosine_table, sine_values_table = rope_tables(own_positions, HEAD_SIZE)
    scale_factor = 1.0 / math.sqrt(HEAD_SIZE)
    half_rows = half_devices * local_rows
    query_positions = lax.dynamic_slice_in_dim(all_positions, my_half * half_rows, half_rows)
    allowed = all_positions[None, :] <= query_positions[:, None]
    half_select = (jnp.arange(halves, dtype=jnp.int32) == my_half)[:, None, None, None]

    def to_heads(per_head):
        by_head = jnp.transpose(per_head, (1, 0, 2))
        return jnp.where(half_select, by_head[None], jnp.zeros_like(by_head)[None]).reshape(
            ctx_size, local_rows, per_head.shape[-1]
        )

    def gather_half(received):
        return lax.dynamic_slice_in_dim(received, my_half * half_devices, half_devices, 0).reshape(
            half_rows, received.shape[-1]
        )

    def from_heads(per_head):
        blocks = per_head.reshape(half_devices, local_rows, per_head.shape[-1])
        return jnp.where(half_select, blocks[None], jnp.zeros_like(blocks)[None]).reshape(
            ctx_size, local_rows, per_head.shape[-1]
        )

    def own_heads(received):
        mine = lax.dynamic_slice_in_dim(received, my_half * half_devices, half_devices, 0)
        return jnp.transpose(mine, (1, 0, 2))

    def exchange(values):
        return lax.all_to_all(values, CTX, split_axis=0, concat_axis=0, tiled=True)

    full_query, full_key, full_value, full_output, full_gate, full_up, full_down = (
        gather_fsdp(query_weight),
        gather_fsdp(key_projection),
        gather_fsdp(value_projection),
        gather_fsdp(output_weight),
        gather_fsdp(gate_weight),
        gather_fsdp(up_weight),
        gather_fsdp(down_weight),
    )
    input_f32 = layer_input[0].astype(jnp.float32)
    gained, first_normed, first_scale = rms_apply(input_f32, first_gain)
    attention_input = gained.astype(jnp.bfloat16)
    query_pre = jnp.dot(attention_input, full_query, preferred_element_type=jnp.float32).reshape(
        local_rows, HQ, HEAD_SIZE
    )
    query_gained, query_normed, query_scale = rms_apply(query_pre, query_gain)
    query_rotated = rotary_apply(query_gained, cosine_table, sine_values_table).astype(jnp.bfloat16)
    key_before_norm = jnp.dot(
        attention_input, full_key, preferred_element_type=jnp.float32
    ).reshape(local_rows, KEY_VALUE_HEADS, HEAD_SIZE)
    key_after_gain, key_after_norm, key_norm_scale = rms_apply(key_before_norm, key_norm_gain)
    own_keys = rotary_apply(key_after_gain, cosine_table, sine_values_table).astype(jnp.bfloat16)
    own_values = (
        jnp.dot(attention_input, full_value, preferred_element_type=jnp.float32)
        .astype(jnp.bfloat16)
        .reshape(local_rows, KEY_VALUE_HEADS, HEAD_SIZE)
    )
    group = HQ // KEY_VALUE_HEADS
    key_value = jnp.repeat(jnp.concatenate([own_keys, own_values], axis=-1), group, axis=1)
    sent = jnp.concatenate(
        [to_heads(query_rotated), jnp.tile(jnp.transpose(key_value, (1, 0, 2)), (halves, 1, 1))],
        axis=-1,
    )
    received = exchange(sent)
    head_query = gather_half(received[..., :HEAD_SIZE])
    head_key = received[..., HEAD_SIZE : 2 * HEAD_SIZE].reshape(-1, HEAD_SIZE)
    head_value = received[..., 2 * HEAD_SIZE :].reshape(-1, HEAD_SIZE)

    def head_scores():
        raw_scores = (
            jnp.einsum("qd,kd->qk", head_query, head_key, preferred_element_type=jnp.float32)
            * scale_factor
        )
        return jnp.where(allowed, raw_scores, MASKED)

    raw_scores = head_scores()
    row_max = jnp.max(raw_scores, axis=-1, keepdims=True)
    log_total = row_max + jnp.log(jnp.sum(jnp.exp(raw_scores - row_max), axis=-1, keepdims=True))
    weights_b = jnp.exp(raw_scores - log_total).astype(jnp.bfloat16)
    head_mixed = jnp.dot(weights_b, head_value, preferred_element_type=jnp.float32)
    mixed_b = own_heads(exchange(from_heads(head_mixed.astype(jnp.bfloat16)))).reshape(
        local_rows, HQ * HEAD_SIZE
    )
    residual_mid = input_f32 + jnp.dot(mixed_b, full_output, preferred_element_type=jnp.float32)
    gained_mid, second_normed, second_scale = rms_apply(residual_mid, second_gain)
    mlp_in = gained_mid.astype(jnp.bfloat16)
    gate_pre = jnp.dot(mlp_in, full_gate, preferred_element_type=jnp.float32)
    up_pre = jnp.dot(mlp_in, full_up, preferred_element_type=jnp.float32)
    sigmoid_gate = jax.nn.sigmoid(gate_pre)
    silu_gate = gate_pre * sigmoid_gate
    hidden = (silu_gate * up_pre).astype(jnp.bfloat16)
    layer_output = (
        residual_mid + jnp.dot(hidden, full_down, preferred_element_type=jnp.float32)
    ).astype(jnp.bfloat16)
    own_cotangent = cotangent[0]
    hidden_grad = right_dot(own_cotangent, full_down)
    gate_grad = (
        hidden_grad * up_pre * sigmoid_gate * (1.0 + gate_pre * (1.0 - sigmoid_gate))
    ).astype(jnp.bfloat16)
    up_grad = (hidden_grad * silu_gate).astype(jnp.bfloat16)
    mlp_in_grad = right_dot(gate_grad, full_gate) + right_dot(up_grad, full_up)
    second_gain_grad = jnp.sum(mlp_in_grad * second_normed, axis=0)
    mid_grad = own_cotangent.astype(jnp.float32) + root_mean_square_backward(
        mlp_in_grad, second_normed, second_scale, second_gain
    )
    mid_grad_b = mid_grad.astype(jnp.bfloat16)
    mixed_gradient = right_dot(mid_grad_b, full_output).astype(jnp.bfloat16)
    head_out_grad = gather_half(
        exchange(to_heads(mixed_gradient.reshape(local_rows, HQ, HEAD_SIZE)))
    )
    out_grad_f = head_out_grad.astype(jnp.float32)
    delta = jnp.sum(out_grad_f * head_mixed, axis=-1, keepdims=True)
    probabilities = jnp.exp(head_scores() - log_total)
    value_part = left_dot(probabilities.astype(jnp.bfloat16), head_out_grad)
    prob_grad = right_dot(head_out_grad, head_value)
    score_grad = (probabilities * (prob_grad - delta)).astype(jnp.bfloat16)
    query_part = jnp.dot(score_grad, head_key, preferred_element_type=jnp.float32) * scale_factor
    key_part = left_dot(score_grad, head_query) * scale_factor
    returned = exchange(
        jnp.concatenate(
            [
                from_heads(query_part.astype(jnp.bfloat16)),
                jnp.concatenate([key_part, value_part], axis=-1)
                .astype(jnp.bfloat16)
                .reshape(ctx_size, local_rows, 2 * HEAD_SIZE),
            ],
            axis=-1,
        )
    )
    query_grad_rows = own_heads(returned[..., :HEAD_SIZE]).astype(jnp.float32)
    kv_parts = (
        returned[..., HEAD_SIZE:]
        .astype(jnp.float32)
        .reshape(halves, KEY_VALUE_HEADS, group, local_rows, 2 * HEAD_SIZE)
    )
    kv_grad = jnp.transpose(jnp.sum(kv_parts, axis=(0, 2)), (1, 0, 2))
    local_key_gradient = kv_grad[..., :HEAD_SIZE]
    own_value_grad = kv_grad[..., HEAD_SIZE:].reshape(local_rows, KEY_VALUE_HEADS * HEAD_SIZE)
    query_back = rotary_backward(query_grad_rows, cosine_table, sine_values_table)
    query_gain_grad = jnp.sum(query_back * query_normed, axis=(0, 1))
    query_pre_grad = (
        root_mean_square_backward(query_back, query_normed, query_scale, query_gain)
        .astype(jnp.bfloat16)
        .reshape(local_rows, HQ * HEAD_SIZE)
    )
    key_backward_pass = rotary_backward(local_key_gradient, cosine_table, sine_values_table)
    key_gain_grad = jnp.sum(key_backward_pass * key_after_norm, axis=(0, 1))
    key_before_norm_gradient = (
        root_mean_square_backward(key_backward_pass, key_after_norm, key_norm_scale, key_norm_gain)
        .astype(jnp.bfloat16)
        .reshape(local_rows, KEY_VALUE_HEADS * HEAD_SIZE)
    )
    value_gradient_second = own_value_grad.astype(jnp.bfloat16)
    attn_in_grad = (
        right_dot(query_pre_grad, full_query)
        + right_dot(key_before_norm_gradient, full_key)
        + right_dot(value_gradient_second, full_value)
    )
    first_gain_grad = jnp.sum(attn_in_grad * first_normed, axis=0)
    input_grad = mid_grad + root_mean_square_backward(
        attn_in_grad, first_normed, first_scale, first_gain
    )
    attn_cols, mixed_cols, mlp_cols, hidden_cols = (
        lax.all_to_all(attention_input, FSDP, split_axis=1, concat_axis=0, tiled=True),
        lax.all_to_all(mixed_b, FSDP, split_axis=1, concat_axis=0, tiled=True),
        lax.all_to_all(mlp_in, FSDP, split_axis=1, concat_axis=0, tiled=True),
        lax.all_to_all(hidden, FSDP, split_axis=1, concat_axis=0, tiled=True),
    )
    cot_rows, gate_rows, up_rows, mid_rows, query_rows, key_rows, value_row_block = (
        gather_fsdp(own_cotangent),
        gather_fsdp(gate_grad),
        gather_fsdp(up_grad),
        gather_fsdp(mid_grad_b),
        gather_fsdp(query_pre_grad),
        gather_fsdp(key_before_norm_gradient),
        gather_fsdp(value_gradient_second),
    )
    query_shard = left_dot(attn_cols, query_rows)
    key_shard = left_dot(attn_cols, key_rows)
    value_shard = left_dot(attn_cols, value_row_block)
    output_shard = left_dot(mixed_cols, mid_rows)
    gate_shard = left_dot(mlp_cols, gate_rows)
    up_shard = left_dot(mlp_cols, up_rows)
    down_shard = left_dot(hidden_cols, cot_rows)
    first_shard, second_shard, query_gain_shard, key_gain_shard = (
        lax.psum_scatter(first_gain_grad, FSDP, scatter_dimension=0, tiled=True),
        lax.psum_scatter(second_gain_grad, FSDP, scatter_dimension=0, tiled=True),
        lax.psum_scatter(query_gain_grad, FSDP, scatter_dimension=0, tiled=True),
        lax.psum_scatter(key_gain_grad, FSDP, scatter_dimension=0, tiled=True),
    )
    shards = (
        query_shard,
        key_shard,
        value_shard,
        output_shard,
        gate_shard,
        up_shard,
        down_shard,
        first_shard,
        second_shard,
        query_gain_shard,
        key_gain_shard,
    )
    totals = reduce_ctx(shards)
    (
        query_total,
        key_total,
        value_total,
        output_total,
        gate_total,
        up_total,
        down_total,
        first_total,
        second_total,
        query_gain_total,
        key_gain_total,
    ) = totals
    return (
        layer_output[None],
        input_grad[None],
        query_total,
        key_total,
        value_total,
        output_total,
        gate_total,
        up_total,
        down_total,
        first_total,
        second_total,
        query_gain_total,
        key_gain_total,
    )


def solution(mesh):
    in_specs = (
        P(FSDP, CTX, None),
        P(FSDP, CTX, None),
        P(FSDP, None),
        P(FSDP, None),
        P(FSDP, None),
        P(FSDP, None),
        P(FSDP, None),
        P(FSDP, None),
        P(FSDP, None),
        P(FSDP, None),
        P(),
        P(),
        P(),
        P(),
    )
    out_specs = (
        P(FSDP, CTX, None),
        P(FSDP, CTX, None),
        P(FSDP, None),
        P(FSDP, None),
        P(FSDP, None),
        P(FSDP, None),
        P(FSDP, None),
        P(FSDP, None),
        P(FSDP, None),
        P(FSDP),
        P(FSDP),
        P(FSDP),
        P(FSDP),
    )
    torus_mesh = jax.sharding.Mesh(mesh.devices.reshape(2, 4, 4, 2, 2), ("yh", "x", "z", "yl", "c"))
    return jax.shard_map(
        on_device, mesh=torus_mesh, in_specs=in_specs, out_specs=out_specs, check_vma=False
    )
```

profile of v0, /device:TPU:1, one launch (start us, length us, event | category | flops | bytes accessed | tf_op | source)
XLA Modules:
  0.0 1240.5 jit_solution(9010868726562113697)
XLA Ops:
  11.2 25.6 %all-gather.61.cloned.1.call-done = bf16[512,1024]{1,0:T(8,128)(2,1)} async-done(((bf16[256,1024]{1,0:T(8,128)(2,1)}), bf16[512,1024]{1,0:T(8,128)(2,1)}) %all-gather.61.cloned.1.call-update) | async-done | bytes 1048592 | tf_op jit(solution)/shard_map/all_gather | solution.py:76
  36.8 26.4 %all-gather.65.cloned.1.call-done = bf16[512,1024]{1,0:T(8,128)(2,1)} async-done(((bf16[256,1024]{1,0:T(8,128)(2,1)}), bf16[512,1024]{1,0:T(8,128)(2,1)}) %all-gather.65.cloned.1.call-update) | async-done | bytes 1048592 | tf_op jit(solution)/shard_map/all_gather | solution.py:76
  63.3 38.2 %all-gather.57.cloned.1.call-done = bf16[512,2048]{1,0:T(8,128)(2,1)} async-done(((bf16[256,2048]{1,0:T(8,128)(2,1)}), bf16[512,2048]{1,0:T(8,128)(2,1)}) %all-gather.57.cloned.1.call-update) | async-done | bytes 2097168 | tf_op jit(solution)/shard_map/all_gather | solution.py:76
  102.2 37.5 %all-gather.69.cloned.1.call-done = bf16[1024,1024]{1,0:T(8,128)(2,1)} async-done(((bf16[512,1024]{1,0:T(8,128)(2,1)}), bf16[1024,1024]{1,0:T(8,128)(2,1)}) %all-gather.69.cloned.1.call-update) | async-done | bytes 2097168 | tf_op jit(solution)/shard_map/all_gather | solution.py:76
  139.8 49.9 %all-gather.73.cloned.1.call-done = bf16[512,3072]{1,0:T(8,128)(2,1)} async-done(((bf16[256,3072]{1,0:T(8,128)(2,1)}), bf16[512,3072]{1,0:T(8,128)(2,1)}) %all-gather.73.cloned.1.call-update) | async-done | bytes 3145744 | tf_op jit(solution)/shard_map/all_gather | solution.py:76
  190.3 49.3 %all-gather.77.cloned.1.call-done = bf16[512,3072]{1,0:T(8,128)(2,1)} async-done(((bf16[256,3072]{1,0:T(8,128)(2,1)}), bf16[512,3072]{1,0:T(8,128)(2,1)}) %all-gather.77.cloned.1.call-update) | async-done | bytes 3145744 | tf_op jit(solution)/shard_map/all_gather | solution.py:76
  239.9 16.1 %all-gather.63.cloned.1.call-done = bf16[2,512,1024]{2,1,0:T(8,128)(2,1)} async-done(((bf16[2,256,1024]{2,1,0:T(8,128)(2,1)}), bf16[2,512,1024]{2,1,0:T(8,128)(2,1)}) %all-gather.63.cloned.1.call-update) | async-done | bytes 2097168 | tf_op jit(solution)/shard_map/all_gather | solution.py:77
  256.0 2.9 copy.80
  261.1 11.2 all-gather.67.cloned.1.call-done
  278.2 13.5 %all-gather.59.cloned.1.call-done = bf16[2,512,2048]{2,1,0:T(8,128)(2,1)} async-done(((bf16[2,256,2048]{2,1,0:T(8,128)(2,1)}), bf16[2,512,2048]{2,1,0:T(8,128)(2,1)}) %all-gather.59.cloned.1.call-update) | async-done | bytes 4194320 | tf_op jit(solution)/shard_map/all_gather | solution.py:77
  291.7 6.4 copy.79
  298.1 3.5 multiply_reduce_fusion.3
  305.8 3.5 pad_maximum_fusion
  309.3 9.6 all-to-all-start
  319.2 56.7 %all-gather.81.cloned.1.call-done = bf16[1536,1024]{1,0:T(8,128)(2,1)} async-done(((bf16[768,1024]{1,0:T(8,128)(2,1)}), bf16[1536,1024]{1,0:T(8,128)(2,1)}) %all-gather.81.cloned.1.call-update) | async-done | bytes 3145744 | tf_op jit(solution)/shard_map/all_gather | solution.py:76
  378.2 14.4 %fusion.49 = (f32[2048]{0:T(1024)S(1)}, f32[2048,4096]{1,0:T(8,128)}) fusion(s32[2048]{0:T(1024)S(1)} %dynamic_slice.18, s32[4096]{0:T(1024)S(1)} %add.146, bf16[2048,128]{1,0:T(8,128)(2,1)S(1)} %bitcast.313, bf16[4096,128]{1,0:T(8,128)(2,1)S(1)} %bitcast.307), kind=kOutput, calls=%fused_computation.148 | convolution fusion | flops 2181036032 | bytes 35160064 | tf_op jit(solution)/shard_map/qd,kd->qk/dot_general | solution.py:199
  392.6 16.1 %exponential_reduce_fusion = f32[2048]{0:T(1024)S(1)} fusion(f32[2048]{0:T(1024)S(1)} %get-tuple-element.56, f32[2048,4096]{1,0:T(8,128)} %get-tuple-element.57, s32[2048]{0:T(1024)S(1)} %dynamic_slice.18, s32[4096]{0:T(1024)S(1)} %add.146), kind=kLoop, calls=%fused_computation.6 | loop fusion | flops 41940992 | bytes 33595392 | tf_op jit(solution)/shard_map/reduce_sum | solution.py:206
  408.7 18.5 %fusion.51 = (bf16[2048,128]{1,0:T(8,128)(2,1)S(1)}, f32[2048,128]{1,0:T(8,128)}) fusion(bf16[4096,128]{1,0:T(8,128)(2,1)S(1)} %bitcast.309, f32[2048]{0:T(1024)S(1)} %log_add_fusion, f32[2048,4096]{1,0:T(8,128)} %get-tuple-element.57, s32[2048]{0:T(1024)S(1)} %dynamic_slice.18, s32[4096]{0:T(1024)S(1)} %add.146), kind=kOutput, calls=%fused_computation.150 | convolution fusion | flops 2189688832 | bytes 36208640 | tf_op jit(solution)/shard_map/dot_general | solution.py:208
  427.6 28.8 %all_to_all.93 = bf16[32,128,128]{1,2,0:T(8,128)(2,1)S(1)} all-to-all(bf16[32,128,128]{1,2,0:T(8,128)(2,1)S(1)} %bitcast_select_fusion.3), channel_id=1, replica_groups=mesh['yh'=2,'x'=4,'z'=4,'yl'=2,'c'=2] {'yh','x','z'}, dimensions={0} | all-to-all | bytes 2097152 | tf_op jit(solution)/shard_map/all_to_all | solution.py:157
  456.5 3.7 multiply_reduce_fusion.8
  460.4 6.0 fusion.52
  466.4 5.0 fusion.53
  471.3 7.5 multiply_convert_fusion.1
  478.9 6.1 fusion.54
  484.9 5.6 multiply_reduce_fusion.5
  497.6 5.5 all-to-all-start.2
  503.5 20.3 %fusion.2 = bf16[4096,2048]{0,1:T(8,128)(2,1)} fusion(f32[2048,4096]{1,0:T(8,128)} %get-tuple-element.57, f32[2048]{0:T(1024)S(1)} %log_add_fusion, s32[4096]{0:T(1024)S(1)} %add.146, s32[2048]{0:T(1024)S(1)} %dynamic_slice.18), kind=kLoop, calls=%fused_computation.3 | loop fusion | flops 41943040 | bytes 50364416 | tf_op jit(solution)/shard_map/convert_element_type | solution.py:207
  523.8 22.6 %copy.81 = bf16[4096,2048]{1,0:T(8,128)(2,1)} copy(bf16[4096,2048]{0,1:T(8,128)(2,1)} %fusion.2) | data formatting | bytes 33554432 | tf_op jit(solution)/shard_map/dot_general | solution.py:64
  551.3 20.5 %multiply_convert_fusion = bf16[2048,4096]{1,0:T(8,128)(2,1)} fusion(f32[2048]{0:T(1024)S(1)} %multiply_reduce_fusion.2, f32[2048]{0:T(1024)S(1)} %log_add_fusion, bf16[2048,128]{1,0:T(8,128)(2,1)S(1)} %bitcast.265, bf16[4096,128]{1,0:T(8,128)(2,1)} %bitcast.310, f32[2048,4096]{1,0:T(8,128)} %get-tuple-element.57, s32[2048]{0:T(1024)S(1)} %dynamic_slice.18, ...), kind=kOutput, calls=%fused_computation.4 | convolution fusion | flops 2206203904 | bytes 51945472 | tf_op jit(solution)/shard_map/dot_general | solution.py:70
  571.7 9.3 fusion.8
  582.7 5.8 fusion.7
  595.0 10.3 convolution_convert_fusion.6
  605.3 3.2 pad_maximum_fusion.1
  608.4 9.3 all-to-all-start.3
  618.4 44.4 %all_gather.212 = bf16[2,128,1024]{2,1,0:T(8,128)(2,1)} all-gather(bf16[1,128,1024]{2,1,0:T(8,128)(2,1)S(1)} %copy-done.15), channel_id=1, replica_groups=mesh['yh'=2,'x'=4,'z'=4,'yl'=2,'c'=2] {'yl'}, dimensions={0}, use_global_device_ids=true | all-gather | bytes 786432 | tf_op jit(solution)/shard_map/all_gather | solution.py:76
  668.0 10.4 all-gather.17
  683.1 6.5 all_gather.194
  691.7 9.3 all-to-all-start.7
  702.2 22.3 %all_gather.197 = bf16[2,128,1024]{2,1,0:T(8,128)(2,1)} all-gather(bf16[1,128,1024]{2,1,0:T(8,128)(2,1)S(1)} %copy.74), channel_id=1, replica_groups=mesh['yh'=2,'x'=4,'z'=4,'yl'=2,'c'=2] {'yl'}, dimensions={0}, use_global_device_ids=true | all-gather | bytes 786432 | tf_op jit(solution)/shard_map/all_gather | solution.py:76
  725.8 6.1 all-to-all-start.5
  735.4 2.5 fusion.12
  740.0 4.2 all-to-all-start.6
  744.2 2.8 all-gather.91.cloned.1.call-done
  754.7 9.4 all-reduce.5
  764.4 5.7 all-to-all-start.4
  770.1 2.9 fusion.10
  774.4 8.2 all-gather.99.cloned.1.call-done
  782.7 2.9 fusion.11
  787.1 10.4 all-gather.87.cloned.1.call-done
  800.0 12.2 all-gather.89.cloned.1.call-done
  815.0 13.3 %all-gather.85.cloned.1.call-done = bf16[2,256,2048]{2,1,0:T(8,128)(2,1)} async-done(((bf16[2,128,2048]{2,1,0:T(8,128)(2,1)}), bf16[2,256,2048]{2,1,0:T(8,128)(2,1)}) %all-gather.85.cloned.1.call-update) | async-done | bytes 2097168 | tf_op jit(solution)/shard_map/all_gather | solution.py:77
  832.0 103.5 %concatenate.38 = bf16[3932736]{0:T(1024)(128)(2,1)} concatenate(bf16[524288]{0:T(1024)(128)(2,1)} %bitcast.272, bf16[262144]{0:T(1024)(128)(2,1)} %bitcast.291, bf16[262144]{0:T(1024)(128)(2,1)} %bitcast.292, bf16[524288]{0:T(1024)(128)(2,1)S(1)} %bitcast.271, bf16[786432]{0:T(1024)(128)(2,1)} %bitcast.261, bf16[786432]{0:T(1024)(128)(2,1)} %bitcast.262, ...), dimensions={0} | concatenate | bytes 15730944 | tf_op jit(solution)/shard_map/concatenate | solution.py:82
  935.5 8.3 pad_bitcast_fusion
  943.9 78.1 %reduce-scatter.3.cloned.1.call-done = bf16[7744,128]{1,0:T(8,128)(2,1)} async-done(((bf16[30976,128]{1,0:T(8,128)(2,1)}), bf16[7744,128]{1,0:T(8,128)(2,1)}) %reduce-scatter.3.cloned.1.call-update) | async-done | bytes 1982480 | tf_op jit(solution)/shard_map/reduce_scatter | solution.py:87
  1022.0 30.6 %reduce-scatter.5.cloned.1.call-done = bf16[1936,128]{1,0:T(8,128)(2,1)} async-done(((bf16[7744,128]{1,0:T(8,128)(2,1)}), bf16[1936,128]{1,0:T(8,128)(2,1)}) %reduce-scatter.5.cloned.1.call-update) | async-done | bytes 495632 | tf_op jit(solution)/shard_map/reduce_scatter | solution.py:88
  1052.7 37.9 %all-reduce.8.cloned.1.call-done = bf16[1936,128]{1,0:T(8,128)(2,1)} async-done(((bf16[1936,128]{1,0:T(8,128)(2,1)}), bf16[1936,128]{1,0:T(8,128)(2,1)}) %all-reduce.8.cloned.1.call-update) | async-done | bytes 495632 | tf_op jit(solution)/shard_map/psum | solution.py:89
  1091.0 31.0 %all-gather.53.cloned.1.call-done = bf16[7744,128]{1,0:T(8,128)(2,1)} async-done(((bf16[1936,128]{1,0:T(8,128)(2,1)}), bf16[7744,128]{1,0:T(8,128)(2,1)}) %all-gather.53.cloned.1.call-update) | async-done | bytes 1982480 | tf_op jit(solution)/shard_map/all_gather | solution.py:90
  1122.0 4.6 fusion.21
  1127.7 75.5 %all-gather.55.cloned.1.call-done = bf16[30976,128]{1,0:T(8,128)(2,1)} async-done(((bf16[7744,128]{1,0:T(8,128)(2,1)}), bf16[30976,128]{1,0:T(8,128)(2,1)}) %all-gather.55.cloned.1.call-update) | async-done | bytes 7929872 | tf_op jit(solution)/shard_map/all_gather | solution.py:91
  1203.3 5.7 slice_convert_fusion
  1208.9 4.5 reshape.471
  1213.4 4.5 reshape.472
  1220.2 3.1 slice_convert_fusion.3
  1223.3 2.7 reshape.467
  (255 shorter events, 91.7 us)
Async XLA Ops:
  7.2 29.6 %all-gather.61.cloned.1.call-start = ((), (), s32[]{:S(2)}) async-start(), calls=%async_computation.18 | async-start | bytes 1572864 | tf_op jit(solution)/shard_map/all_gather | solution.py:76
  7.9 55.3 %all-gather.65.cloned.1.call-start = ((), (), s32[]{:S(2)}) async-start(), calls=%async_computation.20 | async-start | bytes 1572864 | tf_op jit(solution)/shard_map/all_gather | solution.py:76
  8.7 92.9 %all-gather.57.cloned.1.call-start = ((), (), s32[]{:S(2)}) async-start(), calls=%async_computation.16 | async-start | bytes 3145728 | tf_op jit(solution)/shard_map/all_gather | solution.py:76
  9.4 130.3 %all-gather.69.cloned.1.call-start = ((), (), s32[]{:S(2)}) async-start(), calls=%async_computation.22 | async-start | bytes 3145728 | tf_op jit(solution)/shard_map/all_gather | solution.py:76
  10.0 179.7 %all-gather.73.cloned.1.call-start = ((), (), s32[]{:S(2)}) async-start(), calls=%async_computation.24 | async-start | bytes 4718592 | tf_op jit(solution)/shard_map/all_gather | solution.py:76
  10.6 229.1 %all-gather.77.cloned.1.call-start = ((), (), s32[]{:S(2)}) async-start(), calls=%async_computation.26 | async-start | bytes 4718592 | tf_op jit(solution)/shard_map/all_gather | solution.py:76
  11.1 244.9 %all-gather.63.cloned.1.call-start = ((), (), s32[]{:S(2)}) async-start(), calls=%async_computation.19 | async-start | bytes 3145728 | tf_op jit(solution)/shard_map/all_gather | solution.py:77
  36.8 235.6 %all-gather.67.cloned.1.call-start = ((), (), s32[]{:S(2)}) async-start(), calls=%async_computation.21 | async-start | bytes 3145728 | tf_op jit(solution)/shard_map/all_gather | solution.py:77
  63.3 228.5 %all-gather.59.cloned.1.call-start = ((), (), s32[]{:S(2)}) async-start(), calls=%async_computation.17 | async-start | bytes 6291456 | tf_op jit(solution)/shard_map/all_gather | solution.py:77
  101.5 88.4 %copy-start.37 = (s32[1,64]{1,0:T(1,128)S(1)}, s32[1,64]{1,0:T(1,128)}, u32[]{:S(2)}) copy-start(s32[1,64]{1,0:T(1,128)} %param.16) | copy-start | bytes 772
  101.5 88.7 %copy-start = (bf16[1,128,1024]{2,1,0:T(8,128)(2,1)S(1)}, bf16[1,128,1024]{2,1,0:T(8,128)(2,1)}, u32[]{:S(2)}) copy-start(bf16[1,128,1024]{2,1,0:T(8,128)(2,1)} %param.14) | copy-start | bytes 786436
  101.6 274.4 %all-gather.81.cloned.1.call-start = ((), (), s32[]{:S(2)}) async-start(), calls=%async_computation.28 | async-start | bytes 4718592 | tf_op jit(solution)/shard_map/all_gather | solution.py:76
  102.2 354.4 %all-gather.71.cloned.1.call-start = ((), (), s32[]{:S(2)}) async-start(), calls=%async_computation.23 | async-start | bytes 6291456 | tf_op jit(solution)/shard_map/all_gather | solution.py:77
  139.7 320.7 %all-gather.75.cloned.1.call-start = ((), (), s32[]{:S(2)}) async-start(), calls=%async_computation.25 | async-start | bytes 9437184 | tf_op jit(solution)/shard_map/all_gather | solution.py:77
  189.7 69.2 %copy-start.27 = (f32[1024]{0:T(1024)S(1)}, f32[1024]{0:T(1024)}, u32[]{:S(2)}) copy-start(f32[1024]{0:T(1024)} %param.24) | copy-start | bytes 12292
  189.7 276.7 %all-gather.79.cloned.1.call-start = ((), (), s32[]{:S(2)}) async-start(), calls=%async_computation.27 | async-start | bytes 9437184 | tf_op jit(solution)/shard_map/all_gather | solution.py:77
  239.7 20.8 %copy-start.34 = (f32[128]{0:T(128)S(1)}, f32[128]{0:T(128)}, u32[]{:S(2)}) copy-start(f32[128]{0:T(128)} %param.27) | copy-start | bytes 1540
  239.7 58.4 %copy-start.32 = (f32[128]{0:T(128)}, f32[128]{0:T(128)S(1)}, u32[]{:S(2)}) copy-start(f32[128]{0:T(128)S(1)} %add_rsqrt_fusion.3) | copy-start | bytes 1540
  259.7 15.7 %copy-start.30 = (f32[128,8]{0,1:T(8,128)}, f32[128,8]{0,1:T(8,128)S(1)}, u32[]{:S(2)}) copy-start(f32[128,8]{0,1:T(8,128)S(1)} %add_rsqrt_fusion.1) | copy-start | bytes 12292
  309.3 66.7 %all-to-all-start = ((bf16[32,128,384]{2,1,0:T(8,128)(2,1)}), bf16[32,128,384]{2,1,0:T(8,128)(2,1)}, u32[]{:S(2)}, u32[]{:S(2)}) async-start(bf16[32,128,384]{2,1,0:T(8,128)(2,1)} %pad_maximum_fusion), calls=%async_computation | async-start | bytes 6291456 | tf_op jit(solution)/shard_map/all_to_all | solution.py:157
  318.9 152.4 %all-gather.83.cloned.1.call-start = ((), (), s32[]{:S(2)}) async-start(), calls=%async_computation.29 | async-start | bytes 9437184 | tf_op jit(solution)/shard_map/all_gather | solution.py:77
  378.1 14.5 %copy-start.22 = (bf16[32,128,128]{2,1,0:T(8,128)(2,1)}, bf16[32,128,128]{2,1,0:T(8,128)(2,1)S(1)}, u32[]{:S(2)}) copy-start(bf16[32,128,128]{2,1,0:T(8,128)(2,1)S(1)} %get-tuple-element.39) | copy-start | bytes 3145732
  378.1 30.6 %copy-start.24 = (bf16[32,128,128]{2,1,0:T(8,128)(2,1)}, bf16[32,128,128]{2,1,0:T(8,128)(2,1)S(1)}, u32[]{:S(2)}) copy-start(bf16[32,128,128]{2,1,0:T(8,128)(2,1)S(1)} %get-tuple-element.40) | copy-start | bytes 3145732
  378.2 14.4 %copy-start.25 = (bf16[16,128,128]{2,1,0:T(8,128)(2,1)}, bf16[16,128,128]{2,1,0:T(8,128)(2,1)S(1)}, u32[]{:S(2)}) copy-start(bf16[16,128,128]{2,1,0:T(8,128)(2,1)S(1)} %constant_dynamic-slice_fusion.2) | copy-start | bytes 1572868
  427.6 32.6 %copy-start.29 = (f32[1024]{0:T(1024)S(1)}, f32[1024]{0:T(1024)}, u32[]{:S(2)}) copy-start(f32[1024]{0:T(1024)} %param.25) | copy-start | bytes 12292
  466.4 5.0 copy-start.15
  484.9 5.8 copy-start.2
  490.5 4.9 copy-start.9
  497.6 48.9 %all-to-all-start.2 = ((bf16[32,128,128]{1,2,0:T(8,128)(2,1)}), bf16[32,128,128]{1,2,0:T(8,128)(2,1)}, u32[]{:S(2)}, u32[]{:S(2)}) async-start(bf16[32,128,128]{1,2,0:T(8,128)(2,1)} %bitcast_select_fusion.2), calls=%async_computation.2 | async-start | bytes 2097152 | tf_op jit(solution)/shard_map/all_to_all | solution.py:157
  503.1 175.5 %all-gather.93.cloned.1.call-start = ((), (), s32[]{:S(2)}) async-start(), calls=%async_computation.34 | async-start | bytes 2359296 | tf_op jit(solution)/shard_map/all_gather | solution.py:76
  551.3 20.5 %copy-start.23 = (bf16[32,128,128]{2,1,0:T(8,128)(2,1)S(1)}, bf16[32,128,128]{2,1,0:T(8,128)(2,1)}, u32[]{:S(2)}) copy-start(bf16[32,128,128]{2,1,0:T(8,128)(2,1)} %copy-done.22) | copy-start | bytes 3145732
  571.7 9.3 copy-start.26
  571.7 10.9 copy-start.39
  608.4 54.4 %all-to-all-start.3 = ((bf16[32,128,384]{1,2,0:T(8,128)(2,1)}), bf16[32,128,384]{1,2,0:T(8,128)(2,1)}, u32[]{:S(2)}, u32[]{:S(2)}) async-start(bf16[32,128,384]{1,2,0:T(8,128)(2,1)} %pad_maximum_fusion.1), calls=%async_computation.3 | async-start | bytes 6291456 | tf_op jit(solution)/shard_map/all_to_all | solution.py:157
  617.7 61.4 %all-gather.97.cloned.1.call-start = ((), (), s32[]{:S(2)}) async-start(), calls=%async_computation.36 | async-start | bytes 2359296 | tf_op jit(solution)/shard_map/all_gather | solution.py:76
  618.3 117.1 %all-gather.101.cloned.1.call-start = ((), (), s32[]{:S(2)}) async-start(), calls=%async_computation.38 | async-start | bytes 1572864 | tf_op jit(solution)/shard_map/all_gather | solution.py:77
  662.8 76.7 %all-gather.51.cloned.1.call-start = ((), (), s32[]{:S(2)}) async-start(), calls=%async_computation.10 | async-start | bytes 1572864 | tf_op jit(solution)/shard_map/all_gather | solution.py:76
  668.0 79.1 %all-gather.91.cloned.1.call-start = ((), (), s32[]{:S(2)}) async-start(), calls=%async_computation.33 | async-start | bytes 1572864 | tf_op jit(solution)/shard_map/all_gather | solution.py:77
  678.5 91.6 %all-gather.95.cloned.1.call-start = ((), (), s32[]{:S(2)}) async-start(), calls=%async_computation.35 | async-start | bytes 4718592 | tf_op jit(solution)/shard_map/all_gather | solution.py:77
  679.1 103.6 %all-gather.99.cloned.1.call-start = ((), (), s32[]{:S(2)}) async-start(), calls=%async_computation.37 | async-start | bytes 4718592 | tf_op jit(solution)/shard_map/all_gather | solution.py:77
  679.8 117.6 %all-gather.87.cloned.1.call-start = ((), (), s32[]{:S(2)}) async-start(), calls=%async_computation.31 | async-start | bytes 1572864 | tf_op jit(solution)/shard_map/all_gather | solution.py:77
  683.0 41.8 %copy-start.28 = (f32[1024]{0:T(1024)S(1)}, f32[1024]{0:T(1024)}, u32[]{:S(2)}) copy-start(f32[1024]{0:T(1024)} %param.24) | copy-start | bytes 12292
  689.6 42.3 %copy-start.33 = (f32[128]{0:T(128)S(1)}, f32[128]{0:T(128)}, u32[]{:S(2)}) copy-start(f32[128]{0:T(128)} %copy-done.32) | copy-start | bytes 1540
  691.7 41.1 %copy-start.38 = (u32[128]{0:T(128)S(1)}, u32[128]{0:T(128)}, u32[]{:S(2)}) copy-start(u32[128]{0:T(128)} %constant.90) | copy-start | bytes 1540
  691.7 34.1 %all-to-all-start.7 = ((bf16[128,4,768]{2,0,1:T(8,128)(2,1)}), bf16[128,4,768]{2,0,1:T(8,128)(2,1)}, u32[]{:S(2)}, u32[]{:S(2)}) async-start(bf16[128,4,768]{2,0,1:T(8,128)(2,1)} %bitcast.239), calls=%async_computation.7 | async-start | bytes 1572864 | tf_op jit(solution)/shard_map/all_to_all | solution.py:295
  701.0 111.2 %all-gather.89.cloned.1.call-start = ((), (), s32[]{:S(2)}) async-start(), calls=%async_computation.32 | async-start | bytes 1572864 | tf_op jit(solution)/shard_map/all_gather | solution.py:77
  702.1 33.4 %copy-start.19 = (bf16[128,8,128]{0,2,1:T(8,128)(2,1)}, bf16[128,8,128]{0,2,1:T(8,128)(2,1)S(1)}, u32[]{:S(2)}) copy-start(bf16[128,8,128]{0,2,1:T(8,128)(2,1)S(1)} %slice.169) | copy-start | bytes 786436
  725.8 14.2 %all-to-all-start.5 = ((bf16[128,4,512]{2,0,1:T(8,128)(2,1)}), bf16[128,4,512]{2,0,1:T(8,128)(2,1)}, u32[]{:S(2)}, u32[]{:S(2)}) async-start(bf16[128,4,512]{2,0,1:T(8,128)(2,1)} %copy.75), calls=%async_computation.5 | async-start | bytes 1048576 | tf_op jit(solution)/shard_map/all_to_all | solution.py:293
  731.9 96.5 %all-gather.85.cloned.1.call-start = ((), (), s32[]{:S(2)}) async-start(), calls=%async_computation.30 | async-start | bytes 3145728 | tf_op jit(solution)/shard_map/all_gather | solution.py:77
  737.9 12.7 %copy-start.5 = (bf16[2,512,1024]{2,1,0:T(8,128)(2,1)S(1)}, bf16[2,512,1024]{2,1,0:T(8,128)(2,1)}, u32[]{:S(2)}) copy-start(bf16[2,512,1024]{2,1,0:T(8,128)(2,1)} %all-gather.63.cloned.1.call-done) | copy-start | bytes 6291460
  740.0 24.4 %all-to-all-start.6 = ((bf16[128,4,256]{2,0,1:T(8,128)(2,1)}), bf16[128,4,256]{2,0,1:T(8,128)(2,1)S(1)}, u32[]{:S(2)}, u32[]{:S(2)}) async-start(bf16[128,4,256]{2,0,1:T(8,128)(2,1)} %bitcast.306), calls=%async_computation.6 | async-start | bytes 524288 | tf_op jit(solution)/shard_map/all_to_all | solution.py:294
  764.4 22.6 %all-to-all-start.4 = ((bf16[128,4,256]{2,0,1:T(8,128)(2,1)}), bf16[128,4,256]{2,0,1:T(8,128)(2,1)S(1)}, u32[]{:S(2)}, u32[]{:S(2)}) async-start(bf16[128,4,256]{2,0,1:T(8,128)(2,1)} %fusion.24), calls=%async_computation.4 | async-start | bytes 524288 | tf_op jit(solution)/shard_map/all_to_all | solution.py:292
  770.1 251.9 %reduce-scatter.3.cloned.1.call-start = ((), (), s32[]{:S(2)}) async-start(), calls=%async_computation.11 | async-start | bytes 9912320 | tf_op jit(solution)/shard_map/reduce_scatter | solution.py:87
  787.1 25.2 %copy-start.12 = (bf16[128,4,256]{2,0,1:T(8,128)(2,1)}, bf16[128,4,256]{2,0,1:T(8,128)(2,1)S(1)}, u32[]{:S(2)}) copy-start(bf16[128,4,256]{2,0,1:T(8,128)(2,1)S(1)} %all-to-all-done.4) | copy-start | bytes 786436
  812.2 19.8 %copy-start.7 = (bf16[96,8,8,128]{3,1,2,0:T(8,128)(2,1)S(1)}, bf16[96,8,8,128]{3,1,2,0:T(8,128)(2,1)}, u32[]{:S(2)}) copy-start(bf16[96,8,8,128]{3,1,2,0:T(8,128)(2,1)} %copy.93) | copy-start | bytes 4718596
  812.2 19.8 %copy-start.11 = (bf16[64,8,8,128]{3,1,2,0:T(8,128)(2,1)S(1)}, bf16[64,8,8,128]{3,1,2,0:T(8,128)(2,1)}, u32[]{:S(2)}) copy-start(bf16[64,8,8,128]{3,1,2,0:T(8,128)(2,1)} %copy.90) | copy-start | bytes 3145732
  943.8 178.1 %copy-start.14 = (bf16[128,3072]{1,0:T(8,128)(2,1)S(1)}, bf16[128,3072]{1,0:T(8,128)(2,1)}, u32[]{:S(2)}) copy-start(bf16[128,3072]{1,0:T(8,128)(2,1)} %get-tuple-element.38) | copy-start | bytes 2359300
  943.8 108.8 %reduce-scatter.5.cloned.1.call-start = ((), (), s32[]{:S(2)}) async-start(), calls=%async_computation.12 | async-start | bytes 2478080 | tf_op jit(solution)/shard_map/reduce_scatter | solution.py:88
  1022.0 68.6 %all-reduce.8.cloned.1.call-start = ((), (), s32[]{:S(2)}) async-start(), calls=%async_computation.13 | async-start | bytes 991232 | tf_op jit(solution)/shard_map/psum | solution.py:89
  1052.7 69.3 %all-gather.53.cloned.1.call-start = ((), (), s32[]{:S(2)}) async-start(), calls=%async_computation.14 | async-start | bytes 2478080 | tf_op jit(solution)/shard_map/all_gather | solution.py:90
  1090.7 112.6 %all-gather.55.cloned.1.call-start = ((), (), s32[]{:S(2)}) async-start(), calls=%async_computation.15 | async-start | bytes 9912320 | tf_op jit(solution)/shard_map/all_gather | solution.py:91
  1122.0 4.6 copy-start.10
  1122.0 4.6 copy-start.16
  1122.0 4.6 copy-start.21
  (12 other events, 32.1 us)
Sparse Core Ops, SparseCore 0:
  9.7 27.0 all-gather.60
  38.4 24.7 all-gather.64
  64.9 36.6 all-gather.56
  103.0 36.6 all-gather.68
  141.2 48.4 all-gather.72
  191.2 48.4 all-gather.76
  241.3 14.6 all-gather.62
  257.7 14.6 all-gather.66
  274.0 17.6 all-gather.58
  293.2 82.6 all-gather.80
  377.6 21.7 all-gather.70
  400.9 20.8 all-gather.74
  423.4 20.7 all-gather.78
  445.7 20.7 all-gather.82
  546.6 31.9 all-gather.92
  620.5 57.1 all-gather.96
  679.2 15.1 all-gather.100
  696.5 32.6 all-gather.50
  730.9 16.0 all-gather.90
  748.5 16.2 all-gather.94
  766.5 16.1 all-gather.98
  784.3 13.0 all-gather.86
  799.1 13.0 all-gather.88
  813.7 14.6 all-gather.84
  944.0 77.9 reduce-scatter.2
  1024.2 28.3 reduce-scatter.4
  1055.1 35.4 all-reduce.7
  1092.4 29.5 all-gather.52
  1123.7 79.5 all-gather.54
where the time goes:
time: 1260 us; the launch traced here: 1240 us
  waiting for transfers between devices  631 us (50%)
  local copies, waits for them, and re-layouts  204 us (16%)
  matrix products  146 us (12%)
  blocking collectives  122 us (10%)
  other arithmetic  69.1 us (5%)
  starting transfers between devices  51.6 us (4%)
  between operations  16.7 us (1%)
    all_gather x10, waiting for transfers between devices, gather_fsdp(): across = lax.all_gather(values, 'yl', axis=0, tiled=False)  284 us
    concatenate x1, local copies, waits for them, and re-layouts, reduce_ctx(): flat = jnp.concatenate([s.astype(jnp.bfloat16).reshape(-1) for s in shards])  104 us
    all_gather x14, waiting for transfers between devices, gather_fsdp(): both = lax.all_gather(across, 'c', axis=1, tiled=False)  87.8 us
    all_gather x4, blocking collectives, gather_fsdp(): across = lax.all_gather(values, 'yl', axis=0, tiled=False)  83.6 us
    reduce_scatter x1, waiting for transfers between devices, reduce_ctx(): part = lax.psum_scatter(flat, 'z', scatter_dimension=0, tiled=True)  78.1 us
    all_gather x1, waiting for transfers between devices, reduce_ctx(): full = lax.all_gather(part, 'z', axis=0, tiled=True).reshape(-1)  75.5 us
    dot_general x8, matrix products, right_dot(): lax.dot_general(left_side, right_side, (((1,), (1,)), ((), ())), preferre...  45.2 us
    psum x1, waiting for transfers between devices, reduce_ctx(): part = lax.psum(part, 'yh')  37.9 us
  transfers between devices with their start and end apart: 36, of which 21 were waited for; matrix products, arithmetic and copies ran while one was open for 20% of the time, Pallas kernels for 0%

commit v1 on v0

--- a/solution.py
+++ b/solution.py
@@ -88,7 +88,9 @@
     part = lax.psum_scatter(part, "x", scatter_dimension=0, tiled=True)
     part = lax.psum(part, "yh")
     part = lax.all_gather(part, "x", axis=0, tiled=True)
-    full = lax.all_gather(part, "z", axis=0, tiled=True).reshape(-1)
+    full = jnp.concatenate(
+        lax.all_to_all(jnp.stack([part] * lax.axis_size("z")), "z", 0, 0), axis=0
+    ).reshape(-1)
     out = []
     at = 0
     for s in shards:

time: 1260 us -> 1300 us (1.032)
  local copies, waits for them, and re-layouts: 204 us -> 224 us
    all_to_all x0 -> x1, waiting for transfers between devices: none -> 82.5 us  [reduce_ctx(): lax.all_to_all(jnp.stack([part] * lax.axis_size('z')), 'z', 0, 0)]
    all_gather x1 -> x0, waiting for transfers between devices: 75.5 us -> none  [reduce_ctx(): full = lax.all_gather(part, 'z', axis=0, tiled=True).reshape(-1)]
    slice x0 -> x2, local copies, waits for them, and re-layouts: none -> 25.6 us  [reduce_ctx(): out.append(full[at:at + s.size].reshape(s.shape).astype(jnp.float32))]
  transfers between devices with their start and end apart: 36 -> 36, of which waited for: 21 -> 21; matrix products, arithmetic and copies ran while one was open for 20% -> 19% of each run, Pallas kernels for 0% -> 0%
where the time goes in v1:
time: 1300 us; the launch traced here: 1280 us
  waiting for transfers between devices  638 us (49%)
  local copies, waits for them, and re-layouts  224 us (17%)
  matrix products  146 us (11%)
  blocking collectives  122 us (9%)
  other arithmetic  74.7 us (6%)
  starting transfers between devices  57.1 us (4%)
  between operations  16.9 us (1%)
    all_gather x10, waiting for transfers between devices, gather_fsdp(): across = lax.all_gather(values, 'yl', axis=0, tiled=False)  284 us
    concatenate x1, local copies, waits for them, and re-layouts, reduce_ctx(): flat = jnp.concatenate([s.astype(jnp.bfloat16).reshape(-1) for s in shards])  104 us
    all_gather x14, waiting for transfers between devices, gather_fsdp(): both = lax.all_gather(across, 'c', axis=1, tiled=False)  87.8 us
    all_gather x4, blocking collectives, gather_fsdp(): across = lax.all_gather(values, 'yl', axis=0, tiled=False)  83.6 us
    all_to_all x1, waiting for transfers between devices, reduce_ctx(): lax.all_to_all(jnp.stack([part] * lax.axis_size('z')), 'z', 0, 0)  82.5 us
    reduce_scatter x1, waiting for transfers between devices, reduce_ctx(): part = lax.psum_scatter(flat, 'z', scatter_dimension=0, tiled=True)  78.1 us
    dot_general x8, matrix products, right_dot(): lax.dot_general(left_side, right_side, (((1,), (1,)), ((), ())), preferre...  45.2 us
    psum x1, waiting for transfers between devices, reduce_ctx(): part = lax.psum(part, 'yh')  37.7 us
  transfers between devices with their start and end apart: 36, of which 21 were waited for; matrix products, arithmetic and copies ran while one was open for 19% of the time, Pallas kernels for 0%

profile of v1, /device:TPU:1, one launch (start us, length us, event | category | flops | bytes accessed | tf_op | source)
XLA Modules:
  0.0 1279.2 jit_solution(8685085691142303264)
XLA Ops:
  11.2 25.6 %all-gather.58.cloned.1.call-done = bf16[512,1024]{1,0:T(8,128)(2,1)} async-done(((bf16[256,1024]{1,0:T(8,128)(2,1)}), bf16[512,1024]{1,0:T(8,128)(2,1)}) %all-gather.58.cloned.1.call-update) | async-done | bytes 1048592 | tf_op jit(solution)/shard_map/all_gather | solution.py:76
  36.8 26.4 %all-gather.62.cloned.1.call-done = bf16[512,1024]{1,0:T(8,128)(2,1)} async-done(((bf16[256,1024]{1,0:T(8,128)(2,1)}), bf16[512,1024]{1,0:T(8,128)(2,1)}) %all-gather.62.cloned.1.call-update) | async-done | bytes 1048592 | tf_op jit(solution)/shard_map/all_gather | solution.py:76
  63.3 38.2 %all-gather.54.cloned.1.call-done = bf16[512,2048]{1,0:T(8,128)(2,1)} async-done(((bf16[256,2048]{1,0:T(8,128)(2,1)}), bf16[512,2048]{1,0:T(8,128)(2,1)}) %all-gather.54.cloned.1.call-update) | async-done | bytes 2097168 | tf_op jit(solution)/shard_map/all_gather | solution.py:76
  102.2 37.5 %all-gather.66.cloned.1.call-done = bf16[1024,1024]{1,0:T(8,128)(2,1)} async-done(((bf16[512,1024]{1,0:T(8,128)(2,1)}), bf16[1024,1024]{1,0:T(8,128)(2,1)}) %all-gather.66.cloned.1.call-update) | async-done | bytes 2097168 | tf_op jit(solution)/shard_map/all_gather | solution.py:76
  139.8 49.9 %all-gather.70.cloned.1.call-done = bf16[512,3072]{1,0:T(8,128)(2,1)} async-done(((bf16[256,3072]{1,0:T(8,128)(2,1)}), bf16[512,3072]{1,0:T(8,128)(2,1)}) %all-gather.70.cloned.1.call-update) | async-done | bytes 3145744 | tf_op jit(solution)/shard_map/all_gather | solution.py:76
  190.3 49.3 %all-gather.74.cloned.1.call-done = bf16[512,3072]{1,0:T(8,128)(2,1)} async-done(((bf16[256,3072]{1,0:T(8,128)(2,1)}), bf16[512,3072]{1,0:T(8,128)(2,1)}) %all-gather.74.cloned.1.call-update) | async-done | bytes 3145744 | tf_op jit(solution)/shard_map/all_gather | solution.py:76
  239.9 16.1 %all-gather.60.cloned.1.call-done = bf16[2,512,1024]{2,1,0:T(8,128)(2,1)} async-done(((bf16[2,256,1024]{2,1,0:T(8,128)(2,1)}), bf16[2,512,1024]{2,1,0:T(8,128)(2,1)}) %all-gather.60.cloned.1.call-update) | async-done | bytes 2097168 | tf_op jit(solution)/shard_map/all_gather | solution.py:77
  256.0 2.9 copy.80
  261.1 11.2 all-gather.64.cloned.1.call-done
  278.2 13.5 %all-gather.56.cloned.1.call-done = bf16[2,512,2048]{2,1,0:T(8,128)(2,1)} async-done(((bf16[2,256,2048]{2,1,0:T(8,128)(2,1)}), bf16[2,512,2048]{2,1,0:T(8,128)(2,1)}) %all-gather.56.cloned.1.call-update) | async-done | bytes 4194320 | tf_op jit(solution)/shard_map/all_gather | solution.py:77
  291.7 6.4 copy.79
  298.1 3.5 multiply_reduce_fusion.3
  305.8 3.5 pad_maximum_fusion
  309.3 9.6 all-to-all-start
  319.2 56.7 %all-gather.78.cloned.1.call-done = bf16[1536,1024]{1,0:T(8,128)(2,1)} async-done(((bf16[768,1024]{1,0:T(8,128)(2,1)}), bf16[1536,1024]{1,0:T(8,128)(2,1)}) %all-gather.78.cloned.1.call-update) | async-done | bytes 3145744 | tf_op jit(solution)/shard_map/all_gather | solution.py:76
  378.1 14.4 %fusion.47 = (f32[2048]{0:T(1024)S(1)}, f32[2048,4096]{1,0:T(8,128)}) fusion(s32[2048]{0:T(1024)S(1)} %dynamic_slice.18, s32[4096]{0:T(1024)S(1)} %add.146, bf16[2048,128]{1,0:T(8,128)(2,1)S(1)} %bitcast.302, bf16[4096,128]{1,0:T(8,128)(2,1)S(1)} %bitcast.296), kind=kOutput, calls=%fused_computation.146 | convolution fusion | flops 2181036032 | bytes 35160064 | tf_op jit(solution)/shard_map/qd,kd->qk/dot_general | solution.py:201
  392.5 16.1 %exponential_reduce_fusion = f32[2048]{0:T(1024)S(1)} fusion(f32[2048]{0:T(1024)S(1)} %get-tuple-element.53, f32[2048,4096]{1,0:T(8,128)} %get-tuple-element.54, s32[2048]{0:T(1024)S(1)} %dynamic_slice.18, s32[4096]{0:T(1024)S(1)} %add.146), kind=kLoop, calls=%fused_computation.6 | loop fusion | flops 41940992 | bytes 33595392 | tf_op jit(solution)/shard_map/reduce_sum | solution.py:208
  408.6 18.5 %fusion.49 = (bf16[2048,128]{1,0:T(8,128)(2,1)S(1)}, f32[2048,128]{1,0:T(8,128)}) fusion(bf16[4096,128]{1,0:T(8,128)(2,1)S(1)} %bitcast.298, f32[2048]{0:T(1024)S(1)} %log_add_fusion, f32[2048,4096]{1,0:T(8,128)} %get-tuple-element.54, s32[2048]{0:T(1024)S(1)} %dynamic_slice.18, s32[4096]{0:T(1024)S(1)} %add.146), kind=kOutput, calls=%fused_computation.148 | convolution fusion | flops 2189688832 | bytes 36208640 | tf_op jit(solution)/shard_map/dot_general | solution.py:210
  427.5 29.0 %all_to_all.98 = bf16[32,128,128]{1,2,0:T(8,128)(2,1)S(1)} all-to-all(bf16[32,128,128]{1,2,0:T(8,128)(2,1)S(1)} %bitcast_select_fusion.3), channel_id=1, replica_groups=mesh['yh'=2,'x'=4,'z'=4,'yl'=2,'c'=2] {'yh','x','z'}, dimensions={0} | all-to-all | bytes 2097152 | tf_op jit(solution)/shard_map/all_to_all | solution.py:159
  456.5 3.7 multiply_reduce_fusion.8
  460.4 6.0 fusion.50
  466.4 5.0 fusion.51
  471.4 7.5 multiply_convert_fusion.1
  478.9 6.1 fusion.52
  484.9 5.6 multiply_reduce_fusion.5
  497.6 5.5 all-to-all-start.2
  503.5 20.3 %fusion.2 = bf16[4096,2048]{0,1:T(8,128)(2,1)} fusion(f32[2048,4096]{1,0:T(8,128)} %get-tuple-element.54, f32[2048]{0:T(1024)S(1)} %log_add_fusion, s32[4096]{0:T(1024)S(1)} %add.146, s32[2048]{0:T(1024)S(1)} %dynamic_slice.18), kind=kLoop, calls=%fused_computation.3 | loop fusion | flops 41943040 | bytes 50364416 | tf_op jit(solution)/shard_map/convert_element_type | solution.py:209
  523.9 22.6 %copy.81 = bf16[4096,2048]{1,0:T(8,128)(2,1)} copy(bf16[4096,2048]{0,1:T(8,128)(2,1)} %fusion.2) | data formatting | bytes 33554432 | tf_op jit(solution)/shard_map/dot_general | solution.py:64
  551.3 20.5 %multiply_convert_fusion = bf16[2048,4096]{1,0:T(8,128)(2,1)} fusion(f32[2048]{0:T(1024)S(1)} %multiply_reduce_fusion.2, f32[2048]{0:T(1024)S(1)} %log_add_fusion, bf16[2048,128]{1,0:T(8,128)(2,1)S(1)} %bitcast.254, bf16[4096,128]{1,0:T(8,128)(2,1)} %bitcast.299, f32[2048,4096]{1,0:T(8,128)} %get-tuple-element.54, s32[2048]{0:T(1024)S(1)} %dynamic_slice.18, ...), kind=kOutput, calls=%fused_computation.4 | convolution fusion | flops 2206203904 | bytes 51945472 | tf_op jit(solution)/shard_map/dot_general | solution.py:70
  571.7 9.3 fusion.8
  582.6 5.8 fusion.7
  595.0 10.3 convolution_convert_fusion.6
  605.3 3.2 pad_maximum_fusion.1
  608.4 9.3 all-to-all-start.3
  618.4 44.4 %all_gather.209 = bf16[2,128,1024]{2,1,0:T(8,128)(2,1)} all-gather(bf16[1,128,1024]{2,1,0:T(8,128)(2,1)S(1)} %copy-done.15), channel_id=1, replica_groups=mesh['yh'=2,'x'=4,'z'=4,'yl'=2,'c'=2] {'yl'}, dimensions={0}, use_global_device_ids=true | all-gather | bytes 786432 | tf_op jit(solution)/shard_map/all_gather | solution.py:76
  668.0 10.4 all-gather.17
  683.1 6.5 all_gather.191
  691.7 9.3 all-to-all-start.7
  702.2 22.3 %all_gather.194 = bf16[2,128,1024]{2,1,0:T(8,128)(2,1)} all-gather(bf16[1,128,1024]{2,1,0:T(8,128)(2,1)S(1)} %copy.74), channel_id=1, replica_groups=mesh['yh'=2,'x'=4,'z'=4,'yl'=2,'c'=2] {'yl'}, dimensions={0}, use_global_device_ids=true | all-gather | bytes 786432 | tf_op jit(solution)/shard_map/all_gather | solution.py:76
  725.8 6.0 all-to-all-start.5
  740.0 4.2 all-to-all-start.6
  754.7 9.4 all-reduce.5
  764.4 5.7 all-to-all-start.4
  770.1 2.9 fusion.10
  774.4 8.2 all-gather.96.cloned.1.call-done
  782.7 2.9 fusion.11
  787.1 10.4 all-gather.84.cloned.1.call-done
  800.0 12.2 all-gather.86.cloned.1.call-done
  815.1 13.3 %all-gather.82.cloned.1.call-done = bf16[2,256,2048]{2,1,0:T(8,128)(2,1)} async-done(((bf16[2,128,2048]{2,1,0:T(8,128)(2,1)}), bf16[2,256,2048]{2,1,0:T(8,128)(2,1)}) %all-gather.82.cloned.1.call-update) | async-done | bytes 2097168 | tf_op jit(solution)/shard_map/all_gather | solution.py:77
  832.0 103.6 %concatenate.38 = bf16[3932736]{0:T(1024)(128)(2,1)} concatenate(bf16[524288]{0:T(1024)(128)(2,1)} %bitcast.261, bf16[262144]{0:T(1024)(128)(2,1)} %bitcast.280, bf16[262144]{0:T(1024)(128)(2,1)} %bitcast.281, bf16[524288]{0:T(1024)(128)(2,1)S(1)} %bitcast.260, bf16[786432]{0:T(1024)(128)(2,1)} %bitcast.250, bf16[786432]{0:T(1024)(128)(2,1)} %bitcast.251, ...), dimensions={0} | concatenate | bytes 15730944 | tf_op jit(solution)/shard_map/concatenate | solution.py:82
  935.6 8.3 pad_bitcast_fusion
  943.9 78.1 %reduce-scatter.3.cloned.1.call-done = bf16[7744,128]{1,0:T(8,128)(2,1)} async-done(((bf16[30976,128]{1,0:T(8,128)(2,1)}), bf16[7744,128]{1,0:T(8,128)(2,1)}) %reduce-scatter.3.cloned.1.call-update) | async-done | bytes 1982480 | tf_op jit(solution)/shard_map/reduce_scatter | solution.py:87
  1022.1 30.6 %reduce-scatter.5.cloned.1.call-done = bf16[1936,128]{1,0:T(8,128)(2,1)} async-done(((bf16[7744,128]{1,0:T(8,128)(2,1)}), bf16[1936,128]{1,0:T(8,128)(2,1)}) %reduce-scatter.5.cloned.1.call-update) | async-done | bytes 495632 | tf_op jit(solution)/shard_map/reduce_scatter | solution.py:88
  1053.0 37.7 %all-reduce.8.cloned.1.call-done = bf16[1936,128]{1,0:T(8,128)(2,1)} async-done(((bf16[1936,128]{1,0:T(8,128)(2,1)}), bf16[1936,128]{1,0:T(8,128)(2,1)}) %all-reduce.8.cloned.1.call-update) | async-done | bytes 495632 | tf_op jit(solution)/shard_map/psum | solution.py:89
  1090.7 31.3 %all-gather.52.cloned.1.call-done = bf16[7744,128]{1,0:T(8,128)(2,1)} async-done(((bf16[1936,128]{1,0:T(8,128)(2,1)}), bf16[7744,128]{1,0:T(8,128)(2,1)}) %all-gather.52.cloned.1.call-update) | async-done | bytes 1982480 | tf_op jit(solution)/shard_map/all_gather | solution.py:90
  1122.0 5.7 stack.2
  1127.7 5.6 all-to-all-start.8
  1133.4 4.6 fusion.21
  1139.1 82.5 %all-to-all-done.8 = bf16[4,7744,128]{2,1,0:T(8,128)(2,1)} async-done(((bf16[4,7744,128]{2,1,0:T(8,128)(2,1)}), bf16[4,7744,128]{2,1,0:T(8,128)(2,1)}, u32[]{:S(2)}, u32[]{:S(2)}) %all-to-all-start.8) | async-done | bytes 7929888 | tf_op jit(solution)/shard_map/all_to_all | solution.py:92
  1221.6 12.8 %slice.103 = bf16[3872,1024]{1,0:T(8,128)(2,1)} reshape(bf16[4,7744,128]{2,1,0:T(8,128)(2,1)} %all-to-all-done.8) | data formatting | bytes 15859712 | tf_op jit(solution)/shard_map/slice | solution.py:97
  1234.4 3.5 slice_convert_fusion
  1243.4 4.0 slice_convert_fusion.1
  1250.1 12.8 %slice.101 = bf16[1936,2048]{1,0:T(8,128)(2,1)} reshape(bf16[4,7744,128]{2,1,0:T(8,128)(2,1)} %all-to-all-done.8) | data formatting | bytes 15859712 | tf_op jit(solution)/shard_map/slice | solution.py:97
  1265.7 4.5 reshape.445
  (254 shorter events, 99.9 us)
Async XLA Ops:
  7.2 29.6 %all-gather.58.cloned.1.call-start = ((), (), s32[]{:S(2)}) async-start(), calls=%async_computation.18 | async-start | bytes 1572864 | tf_op jit(solution)/shard_map/all_gather | solution.py:76
  7.9 55.3 %all-gather.62.cloned.1.call-start = ((), (), s32[]{:S(2)}) async-start(), calls=%async_computation.20 | async-start | bytes 1572864 | tf_op jit(solution)/shard_map/all_gather | solution.py:76
  8.7 92.9 %all-gather.54.cloned.1.call-start = ((), (), s32[]{:S(2)}) async-start(), calls=%async_computation.16 | async-start | bytes 3145728 | tf_op jit(solution)/shard_map/all_gather | solution.py:76
  9.4 130.3 %all-gather.66.cloned.1.call-start = ((), (), s32[]{:S(2)}) async-start(), calls=%async_computation.22 | async-start | bytes 3145728 | tf_op jit(solution)/shard_map/all_gather | solution.py:76
  10.0 179.7 %all-gather.70.cloned.1.call-start = ((), (), s32[]{:S(2)}) async-start(), calls=%async_computation.24 | async-start | bytes 4718592 | tf_op jit(solution)/shard_map/all_gather | solution.py:76
  10.6 229.1 %all-gather.74.cloned.1.call-start = ((), (), s32[]{:S(2)}) async-start(), calls=%async_computation.26 | async-start | bytes 4718592 | tf_op jit(solution)/shard_map/all_gather | solution.py:76
  11.1 244.9 %all-gather.60.cloned.1.call-start = ((), (), s32[]{:S(2)}) async-start(), calls=%async_computation.19 | async-start | bytes 3145728 | tf_op jit(solution)/shard_map/all_gather | solution.py:77
  36.8 235.6 %all-gather.64.cloned.1.call-start = ((), (), s32[]{:S(2)}) async-start(), calls=%async_computation.21 | async-start | bytes 3145728 | tf_op jit(solution)/shard_map/all_gather | solution.py:77
  63.3 228.5 %all-gather.56.cloned.1.call-start = ((), (), s32[]{:S(2)}) async-start(), calls=%async_computation.17 | async-start | bytes 6291456 | tf_op jit(solution)/shard_map/all_gather | solution.py:77
  101.5 88.4 %copy-start.37 = (s32[1,64]{1,0:T(1,128)S(1)}, s32[1,64]{1,0:T(1,128)}, u32[]{:S(2)}) copy-start(s32[1,64]{1,0:T(1,128)} %param.16) | copy-start | bytes 772
  101.5 88.7 %copy-start = (bf16[1,128,1024]{2,1,0:T(8,128)(2,1)S(1)}, bf16[1,128,1024]{2,1,0:T(8,128)(2,1)}, u32[]{:S(2)}) copy-start(bf16[1,128,1024]{2,1,0:T(8,128)(2,1)} %param.14) | copy-start | bytes 786436
  101.6 274.3 %all-gather.78.cloned.1.call-start = ((), (), s32[]{:S(2)}) async-start(), calls=%async_computation.28 | async-start | bytes 4718592 | tf_op jit(solution)/shard_map/all_gather | solution.py:76
  102.2 354.4 %all-gather.68.cloned.1.call-start = ((), (), s32[]{:S(2)}) async-start(), calls=%async_computation.23 | async-start | bytes 6291456 | tf_op jit(solution)/shard_map/all_gather | solution.py:77
  139.7 320.7 %all-gather.72.cloned.1.call-start = ((), (), s32[]{:S(2)}) async-start(), calls=%async_computation.25 | async-start | bytes 9437184 | tf_op jit(solution)/shard_map/all_gather | solution.py:77
  189.7 69.2 %copy-start.27 = (f32[1024]{0:T(1024)S(1)}, f32[1024]{0:T(1024)}, u32[]{:S(2)}) copy-start(f32[1024]{0:T(1024)} %param.24) | copy-start | bytes 12292
  189.7 276.7 %all-gather.76.cloned.1.call-start = ((), (), s32[]{:S(2)}) async-start(), calls=%async_computation.27 | async-start | bytes 9437184 | tf_op jit(solution)/shard_map/all_gather | solution.py:77
  239.7 20.8 %copy-start.34 = (f32[128]{0:T(128)S(1)}, f32[128]{0:T(128)}, u32[]{:S(2)}) copy-start(f32[128]{0:T(128)} %param.27) | copy-start | bytes 1540
  239.7 58.4 %copy-start.32 = (f32[128]{0:T(128)}, f32[128]{0:T(128)S(1)}, u32[]{:S(2)}) copy-start(f32[128]{0:T(128)S(1)} %add_rsqrt_fusion.3) | copy-start | bytes 1540
  259.7 15.7 %copy-start.30 = (f32[128,8]{0,1:T(8,128)}, f32[128,8]{0,1:T(8,128)S(1)}, u32[]{:S(2)}) copy-start(f32[128,8]{0,1:T(8,128)S(1)} %add_rsqrt_fusion.1) | copy-start | bytes 12292
  309.3 66.6 %all-to-all-start = ((bf16[32,128,384]{2,1,0:T(8,128)(2,1)}), bf16[32,128,384]{2,1,0:T(8,128)(2,1)}, u32[]{:S(2)}, u32[]{:S(2)}) async-start(bf16[32,128,384]{2,1,0:T(8,128)(2,1)} %pad_maximum_fusion), calls=%async_computation | async-start | bytes 6291456 | tf_op jit(solution)/shard_map/all_to_all | solution.py:159
  318.9 152.4 %all-gather.80.cloned.1.call-start = ((), (), s32[]{:S(2)}) async-start(), calls=%async_computation.29 | async-start | bytes 9437184 | tf_op jit(solution)/shard_map/all_gather | solution.py:77
  378.0 14.5 %copy-start.22 = (bf16[32,128,128]{2,1,0:T(8,128)(2,1)}, bf16[32,128,128]{2,1,0:T(8,128)(2,1)S(1)}, u32[]{:S(2)}) copy-start(bf16[32,128,128]{2,1,0:T(8,128)(2,1)S(1)} %get-tuple-element.36) | copy-start | bytes 3145732
  378.0 30.5 %copy-start.24 = (bf16[32,128,128]{2,1,0:T(8,128)(2,1)}, bf16[32,128,128]{2,1,0:T(8,128)(2,1)S(1)}, u32[]{:S(2)}) copy-start(bf16[32,128,128]{2,1,0:T(8,128)(2,1)S(1)} %get-tuple-element.37) | copy-start | bytes 3145732
  378.1 14.4 %copy-start.25 = (bf16[16,128,128]{2,1,0:T(8,128)(2,1)}, bf16[16,128,128]{2,1,0:T(8,128)(2,1)S(1)}, u32[]{:S(2)}) copy-start(bf16[16,128,128]{2,1,0:T(8,128)(2,1)S(1)} %constant_dynamic-slice_fusion.2) | copy-start | bytes 1572868
  427.5 32.7 %copy-start.29 = (f32[1024]{0:T(1024)S(1)}, f32[1024]{0:T(1024)}, u32[]{:S(2)}) copy-start(f32[1024]{0:T(1024)} %param.25) | copy-start | bytes 12292
  466.4 5.0 copy-start.15
  484.9 5.8 copy-start.2
  490.5 4.9 copy-start.9
  497.6 48.9 %all-to-all-start.2 = ((bf16[32,128,128]{1,2,0:T(8,128)(2,1)}), bf16[32,128,128]{1,2,0:T(8,128)(2,1)}, u32[]{:S(2)}, u32[]{:S(2)}) async-start(bf16[32,128,128]{1,2,0:T(8,128)(2,1)} %bitcast_select_fusion.2), calls=%async_computation.2 | async-start | bytes 2097152 | tf_op jit(solution)/shard_map/all_to_all | solution.py:159
  503.1 175.5 %all-gather.90.cloned.1.call-start = ((), (), s32[]{:S(2)}) async-start(), calls=%async_computation.34 | async-start | bytes 2359296 | tf_op jit(solution)/shard_map/all_gather | solution.py:76
  551.2 20.5 %copy-start.23 = (bf16[32,128,128]{2,1,0:T(8,128)(2,1)S(1)}, bf16[32,128,128]{2,1,0:T(8,128)(2,1)}, u32[]{:S(2)}) copy-start(bf16[32,128,128]{2,1,0:T(8,128)(2,1)} %copy-done.22) | copy-start | bytes 3145732
  571.7 9.3 copy-start.26
  571.7 10.9 copy-start.39
  608.4 54.4 %all-to-all-start.3 = ((bf16[32,128,384]{1,2,0:T(8,128)(2,1)}), bf16[32,128,384]{1,2,0:T(8,128)(2,1)}, u32[]{:S(2)}, u32[]{:S(2)}) async-start(bf16[32,128,384]{1,2,0:T(8,128)(2,1)} %pad_maximum_fusion.1), calls=%async_computation.3 | async-start | bytes 6291456 | tf_op jit(solution)/shard_map/all_to_all | solution.py:159
  617.7 61.4 %all-gather.94.cloned.1.call-start = ((), (), s32[]{:S(2)}) async-start(), calls=%async_computation.36 | async-start | bytes 2359296 | tf_op jit(solution)/shard_map/all_gather | solution.py:76
  618.3 117.1 %all-gather.98.cloned.1.call-start = ((), (), s32[]{:S(2)}) async-start(), calls=%async_computation.38 | async-start | bytes 1572864 | tf_op jit(solution)/shard_map/all_gather | solution.py:77
  662.8 76.7 %all-gather.50.cloned.1.call-start = ((), (), s32[]{:S(2)}) async-start(), calls=%async_computation.11 | async-start | bytes 1572864 | tf_op jit(solution)/shard_map/all_gather | solution.py:76
  668.0 79.1 %all-gather.88.cloned.1.call-start = ((), (), s32[]{:S(2)}) async-start(), calls=%async_computation.33 | async-start | bytes 1572864 | tf_op jit(solution)/shard_map/all_gather | solution.py:77
  678.5 91.6 %all-gather.92.cloned.1.call-start = ((), (), s32[]{:S(2)}) async-start(), calls=%async_computation.35 | async-start | bytes 4718592 | tf_op jit(solution)/shard_map/all_gather | solution.py:77
  679.0 103.6 %all-gather.96.cloned.1.call-start = ((), (), s32[]{:S(2)}) async-start(), calls=%async_computation.37 | async-start | bytes 4718592 | tf_op jit(solution)/shard_map/all_gather | solution.py:77
  679.8 117.6 %all-gather.84.cloned.1.call-start = ((), (), s32[]{:S(2)}) async-start(), calls=%async_computation.31 | async-start | bytes 1572864 | tf_op jit(solution)/shard_map/all_gather | solution.py:77
  682.9 41.9 %copy-start.28 = (f32[1024]{0:T(1024)S(1)}, f32[1024]{0:T(1024)}, u32[]{:S(2)}) copy-start(f32[1024]{0:T(1024)} %param.24) | copy-start | bytes 12292
  689.6 42.3 %copy-start.33 = (f32[128]{0:T(128)S(1)}, f32[128]{0:T(128)}, u32[]{:S(2)}) copy-start(f32[128]{0:T(128)} %copy-done.32) | copy-start | bytes 1540
  691.7 41.1 %copy-start.38 = (u32[128]{0:T(128)S(1)}, u32[128]{0:T(128)}, u32[]{:S(2)}) copy-start(u32[128]{0:T(128)} %constant.90) | copy-start | bytes 1540
  691.7 34.1 %all-to-all-start.7 = ((bf16[128,4,768]{2,0,1:T(8,128)(2,1)}), bf16[128,4,768]{2,0,1:T(8,128)(2,1)}, u32[]{:S(2)}, u32[]{:S(2)}) async-start(bf16[128,4,768]{2,0,1:T(8,128)(2,1)} %bitcast.229), calls=%async_computation.7 | async-start | bytes 1572864 | tf_op jit(solution)/shard_map/all_to_all | solution.py:297
  701.0 111.2 %all-gather.86.cloned.1.call-start = ((), (), s32[]{:S(2)}) async-start(), calls=%async_computation.32 | async-start | bytes 1572864 | tf_op jit(solution)/shard_map/all_gather | solution.py:77
  702.1 33.3 %copy-start.19 = (bf16[128,8,128]{0,2,1:T(8,128)(2,1)}, bf16[128,8,128]{0,2,1:T(8,128)(2,1)S(1)}, u32[]{:S(2)}) copy-start(bf16[128,8,128]{0,2,1:T(8,128)(2,1)S(1)} %slice.167) | copy-start | bytes 786436
  725.8 14.1 %all-to-all-start.5 = ((bf16[128,4,512]{2,0,1:T(8,128)(2,1)}), bf16[128,4,512]{2,0,1:T(8,128)(2,1)}, u32[]{:S(2)}, u32[]{:S(2)}) async-start(bf16[128,4,512]{2,0,1:T(8,128)(2,1)} %copy.75), calls=%async_computation.5 | async-start | bytes 1048576 | tf_op jit(solution)/shard_map/all_to_all | solution.py:295
  731.9 96.5 %all-gather.82.cloned.1.call-start = ((), (), s32[]{:S(2)}) async-start(), calls=%async_computation.30 | async-start | bytes 3145728 | tf_op jit(solution)/shard_map/all_gather | solution.py:77
  737.9 12.7 copy-start.5
  740.0 24.5 %all-to-all-start.6 = ((bf16[128,4,256]{2,0,1:T(8,128)(2,1)}), bf16[128,4,256]{2,0,1:T(8,128)(2,1)S(1)}, u32[]{:S(2)}, u32[]{:S(2)}) async-start(bf16[128,4,256]{2,0,1:T(8,128)(2,1)} %bitcast.295), calls=%async_computation.6 | async-start | bytes 524288 | tf_op jit(solution)/shard_map/all_to_all | solution.py:296
  764.4 22.6 %all-to-all-start.4 = ((bf16[128,4,256]{2,0,1:T(8,128)(2,1)}), bf16[128,4,256]{2,0,1:T(8,128)(2,1)S(1)}, u32[]{:S(2)}, u32[]{:S(2)}) async-start(bf16[128,4,256]{2,0,1:T(8,128)(2,1)} %fusion.24), calls=%async_computation.4 | async-start | bytes 524288 | tf_op jit(solution)/shard_map/all_to_all | solution.py:294
  770.1 251.9 %reduce-scatter.3.cloned.1.call-start = ((), (), s32[]{:S(2)}) async-start(), calls=%async_computation.12 | async-start | bytes 9912320 | tf_op jit(solution)/shard_map/reduce_scatter | solution.py:87
  787.1 25.2 %copy-start.12 = (bf16[128,4,256]{2,0,1:T(8,128)(2,1)}, bf16[128,4,256]{2,0,1:T(8,128)(2,1)S(1)}, u32[]{:S(2)}) copy-start(bf16[128,4,256]{2,0,1:T(8,128)(2,1)S(1)} %all-to-all-done.4) | copy-start | bytes 786436
  812.2 19.8 %copy-start.7 = (bf16[96,8,8,128]{3,1,2,0:T(8,128)(2,1)S(1)}, bf16[96,8,8,128]{3,1,2,0:T(8,128)(2,1)}, u32[]{:S(2)}) copy-start(bf16[96,8,8,128]{3,1,2,0:T(8,128)(2,1)} %copy.93) | copy-start | bytes 4718596
  812.2 19.8 %copy-start.11 = (bf16[64,8,8,128]{3,1,2,0:T(8,128)(2,1)S(1)}, bf16[64,8,8,128]{3,1,2,0:T(8,128)(2,1)}, u32[]{:S(2)}) copy-start(bf16[64,8,8,128]{3,1,2,0:T(8,128)(2,1)} %copy.90) | copy-start | bytes 3145732
  943.9 108.8 %reduce-scatter.5.cloned.1.call-start = ((), (), s32[]{:S(2)}) async-start(), calls=%async_computation.13 | async-start | bytes 2478080 | tf_op jit(solution)/shard_map/reduce_scatter | solution.py:88
  1022.0 68.6 %all-reduce.8.cloned.1.call-start = ((), (), s32[]{:S(2)}) async-start(), calls=%async_computation.14 | async-start | bytes 991232 | tf_op jit(solution)/shard_map/psum | solution.py:89
  1052.7 69.3 %all-gather.52.cloned.1.call-start = ((), (), s32[]{:S(2)}) async-start(), calls=%async_computation.15 | async-start | bytes 2478080 | tf_op jit(solution)/shard_map/all_gather | solution.py:90
  1127.7 5.7 copy-start.14
  1127.7 93.9 %all-to-all-start.8 = ((bf16[4,7744,128]{2,1,0:T(8,128)(2,1)}), bf16[4,7744,128]{2,1,0:T(8,128)(2,1)}, u32[]{:S(2)}, u32[]{:S(2)}) async-start(bf16[4,7744,128]{2,1,0:T(8,128)(2,1)} %stack.2), calls=%async_computation.10 | async-start | bytes 15859712 | tf_op jit(solution)/shard_map/all_to_all | solution.py:92
  1133.3 4.6 copy-start.10
  1133.3 4.6 copy-start.16
  1133.3 4.6 copy-start.21
  (12 other events, 32.1 us)
Sparse Core Ops, SparseCore 0:
  9.7 27.0 all-gather.57
  38.4 24.7 all-gather.61
  64.9 36.6 all-gather.53
  103.0 36.6 all-gather.65
  141.2 48.4 all-gather.69
  191.2 48.4 all-gather.73
  241.3 14.6 all-gather.59
  257.7 14.6 all-gather.63
  274.0 17.6 all-gather.55
  293.2 82.5 all-gather.77
  377.5 21.7 all-gather.67
  400.9 20.8 all-gather.71
  423.4 20.7 all-gather.75
  445.7 20.7 all-gather.79
  546.6 31.9 all-gather.89
  620.5 57.1 all-gather.93
  679.2 15.2 all-gather.97
  696.5 32.6 all-gather.49
  730.9 16.0 all-gather.87
  748.5 16.2 all-gather.91
  766.5 16.1 all-gather.95
  784.3 13.0 all-gather.83
  799.1 13.0 all-gather.85
  813.7 14.6 all-gather.81
  944.0 77.9 reduce-scatter.2
  1024.3 28.3 reduce-scatter.4
  1055.1 35.4 all-reduce.7
  1092.4 29.5 all-gather.51
